TPU v7x, 128 devices: a whole 4x4x4 slice. The times are simulated.
128 devices in a mesh: span: 16 (over z, y_lo, core), wall: 8 (over y_hi, x).
Axes of the slice: x: 4, y: 4 (y_hi: 2, y_lo: 2; y = y_hi * 2 + y_lo), z: 4, core: 2. Of those that a mesh axis runs over, the one named last changes fastest.
Arguments:
- noise: bfloat16 [3, 32, 512, 2048], P(None, None, 'wall', 'span'), may hold values from -6 to 6
- wall_scale: float32 [3], replicated, may hold values from 4 to 12
- span_scale: float32 [3], replicated, may hold values from 4 to 12
- lund_factor: float32 [6, 512], P(None, 'wall'), may hold values from 0.2 to 1
- mean_velocity: float32 [512], P('wall'), may hold values from 0.2 to 1
- owner_map: int32 [8, 16, 512, 1], P('wall', 'span'), may hold values from 0 to 127; in each aligned block of 512 rows (0 to 511, 512 to 1023, ..., all dimensions but the last counted through in order) at most 8 rows name the same one
Outputs:
- face_state: bfloat16 [128, 1024, 1536], P(('span', 'wall'))
Inputs may be any that keep to these rules, and one draw needn't show every extreme that they name: `owner_map`: within one tile no owner receives more than 8 elements, and in every draw some tile sends exactly 8 elements to some owner; every device owns some element.
All inputs are finite; a program needn't handle non-finite values.
Results may differ from a plain program's by a relative error of at most 0.001.
Values may be sent and summed in bfloat16 or wider, within the bound.
A program may use at most 64 MiB of HBM per device.

v0:
```python
import math

import jax
import jax.numpy as jnp
from jax import lax
from jax.sharding import PartitionSpec as P

HALO = 24
EDGE = 4


def with_halo(block, sides, width, periodic):
    for axis, dim in sides:
        count = lax.axis_size(axis)
        forward = [(i, i + 1) for i in range(count - 1)]
        if periodic:
            forward.append((count - 1, 0))
        backward = [(target, source) for source, target in forward]
        low = lax.ppermute(
            lax.slice_in_dim(block, block.shape[dim] - width, None, axis=dim), axis, forward
        )
        high = lax.ppermute(lax.slice_in_dim(block, 0, width, axis=dim), axis, backward)
        block = jnp.concatenate([low, block, high], axis=dim)
    return block


def band_matrix(scale, rows):
    row_ids = jnp.arange(rows)[:, None]
    col_ids = jnp.arange(rows + 2 * HALO)[None, :]
    offset = (col_ids - row_ids).astype(jnp.float32)
    valid = (col_ids - row_ids >= 0) & (col_ids - row_ids <= 2 * HALO)
    taps_axis = jnp.arange(-HALO, HALO + 1).astype(jnp.float32)
    norms = jnp.sqrt(
        jnp.sum(jnp.exp(-math.pi * taps_axis[None, :] ** 2 / scale[:, None] ** 2), axis=1)
    )
    shifted = offset[None] - HALO
    values = jnp.exp(
        -math.pi * shifted * shifted / (2.0 * scale[:, None, None] * scale[:, None, None])
    )
    return jnp.where(valid[None], values, 0.0) / norms[:, None, None]


def wall_pass(extended, matrix):
    return jnp.einsum(
        "cij,ctjz->ctiz", matrix, extended.astype(jnp.float32), precision=lax.Precision.HIGHEST
    )


def span_pass(extended, matrix):
    return jnp.einsum("ctyk,czk->ctyz", extended, matrix, precision=lax.Precision.HIGHEST)


def per_device(noise, wall_scale, span_scale, lund_factor, mean_velocity, owner_map):
    trio, planes, rows, cols = noise.shape
    wall_matrix = band_matrix(wall_scale, rows)
    span_matrix = band_matrix(span_scale, cols)
    tall = with_halo(noise, (("wall", 2),), HALO, False)
    smooth = wall_pass(tall, wall_matrix)
    broad = with_halo(smooth, (("span", 3),), HALO, True)
    psi = span_pass(broad, span_matrix)
    factor = lund_factor[:, None, :, None]
    along = mean_velocity[None, :, None] + factor[0] * psi[0]
    normal = factor[1] * psi[0] + factor[2] * psi[1]
    spanwise = factor[3] * psi[0] + factor[4] * psi[1] + factor[5] * psi[2]
    velocity = jnp.stack([along, normal, spanwise]).astype(jnp.bfloat16)
    blocks = velocity.reshape(3, planes, rows // EDGE, EDGE, cols // EDGE, EDGE)
    payload = jnp.transpose(blocks, (2, 4, 0, 1, 3, 5)).reshape(-1, 3 * planes * EDGE * EDGE)
    elements = payload.shape[0]
    n_span = lax.axis_size("span")
    n_wall = lax.axis_size("wall")
    devices = n_span * n_wall
    slots = max(8, 2 * elements // devices)
    owners = owner_map.reshape(elements)
    onehot = (owners[:, None] == jnp.arange(devices, dtype=jnp.int32)[None, :]).astype(jnp.int32)
    rank = jnp.sum(onehot * (jnp.cumsum(onehot, axis=0) - 1), axis=1)
    target = owners * slots + rank
    outgoing = jnp.zeros((devices * slots, payload.shape[1]), jnp.bfloat16).at[target].set(payload)
    received = lax.all_to_all(
        outgoing.reshape(devices, slots, payload.shape[1]),
        ("span", "wall"),
        split_axis=0,
        concat_axis=0,
        tiled=True,
    )
    return received.reshape(1, devices * slots, payload.shape[1])


def solution(mesh):
    return jax.shard_map(
        per_device,
        mesh=mesh,
        in_specs=(
            P(None, None, "wall", "span"),
            P(),
            P(),
            P(None, "wall"),
            P("wall"),
            P("wall", "span", None, None),
        ),
        out_specs=P(("span", "wall"), None, None),
        check_vma=False,
    )
```

profile of v0, /device:TPU:1, one launch (start us, length us, event | category | flops | bytes accessed | tf_op | source)
XLA Modules:
  0.0 178.0 jit_solution(14009626019967277402)
XLA Ops:
  0.0 1.5 fusion.54
  1.5 4.0 %collective-permute-start = (bf16[3,32,24,128]{3,2,1,0:T(8,128)(2,1)S(1)}, bf16[3,32,24,128]{3,2,1,0:T(8,128)(2,1)S(1)}, u32[]{:S(2)}, u32[]{:S(2)}) collective-permute-start(bf16[3,32,24,128]{3,2,1,0:T(8,128)(2,1)S(1)} %get-tuple-element.12), channel_id=1, source_target_pairs={{0,1},{1,2},{2,3},{3,4},{4,5},{5,6},{6,7},{8,9},{9,10},{10,11},{11... | collective-permute-start | bytes 1769480 | tf_op jit(solution)/shard_map/ppermute | solution.py:19
  8.9 8.5 %collective-permute-done = bf16[3,32,24,128]{3,2,1,0:T(8,128)(2,1)S(1)} collective-permute-done((bf16[3,32,24,128]{3,2,1,0:T(8,128)(2,1)S(1)}, bf16[3,32,24,128]{3,2,1,0:T(8,128)(2,1)S(1)}, u32[]{:S(2)}, u32[]{:S(2)}) %collective-permute-start) | collective-permute-done | bytes 589856 | tf_op jit(solution)/shard_map/ppermute | solution.py:19
  17.4 3.8 %collective-permute-done.1 = bf16[3,32,24,128]{3,2,1,0:T(8,128)(2,1)S(1)} collective-permute-done((bf16[3,32,24,128]{3,2,1,0:T(8,128)(2,1)S(1)}, bf16[3,32,24,128]{3,2,1,0:T(8,128)(2,1)S(1)}, u32[]{:S(2)}, u32[]{:S(2)}) %collective-permute-start.1) | collective-permute-done | bytes 589856 | tf_op jit(solution)/shard_map/ppermute | solution.py:22
  22.0 3.2 %fusion.12 = f32[3,32,64,128]{3,2,1,0:T(8,128)S(1)} fusion(bf16[3,32,24,128]{3,2,1,0:T(8,128)(2,1)} %copy-done.4, bf16[3,32,64,128]{3,2,1,0:T(8,128)(2,1)} %param.6, bf16[3,32,24,128]{3,2,1,0:T(8,128)(2,1)} %copy-done.3, f32[3]{0:T(128)S(1)} %sqrt.14, f32[3]{0:T(128)S(1)} %get-tuple-element.25, f32[64,112]{1,0:T(8,128)S(1)} %multiply_multiply_fusion.1, ...), kind=kOutput, calls=%fused_computation.14 | convolution fusion | flops 1065286656 | bytes 5934104 | tf_op jit(solution)/shard_map/cij,ctjz->ctiz/dot_general | solution.py:44
  25.2 3.8 %fusion.53 = (f32[3,32,64,24]{3,2,1,0:T(8,128)}, f32[3,32,64,24]{3,2,1,0:T(8,128)}) fusion(f32[3,32,64,128]{3,2,1,0:T(8,128)S(1)} %fusion.12), kind=kLoop, calls=%fused_computation.78 | loop fusion | bytes 2359296 | tf_op jit(solution)/shard_map/slice | solution.py:20
  29.0 3.2 %copy.34 = f32[3,32,64,24]{2,3,1,0:T(8,128)} copy(f32[3,32,64,24]{3,2,1,0:T(8,128)} %get-tuple-element.10) | data formatting | bytes 1179648 | tf_op jit(solution)/shard_map/slice | solution.py:20
  32.2 3.0 %collective-permute-start.2 = (f32[3,32,64,24]{2,3,1,0:T(8,128)}, f32[3,32,64,24]{2,3,1,0:T(8,128)}, u32[]{:S(2)}, u32[]{:S(2)}) collective-permute-start(f32[3,32,64,24]{2,3,1,0:T(8,128)} %copy.34), channel_id=1, source_target_pairs={{0,8},{8,16},{16,24},{24,32},{32,40},{40,48},{48,56},{56,64},{64,7... | collective-permute-start | bytes 1769480 | tf_op jit(solution)/shard_map/ppermute | solution.py:19
  35.3 3.2 %copy.35 = f32[3,32,64,24]{2,3,1,0:T(8,128)} copy(f32[3,32,64,24]{3,2,1,0:T(8,128)} %get-tuple-element.11) | data formatting | bytes 1179648 | tf_op jit(solution)/shard_map/slice | solution.py:22
  38.8 16.5 %collective-permute-done.2 = f32[3,32,64,24]{2,3,1,0:T(8,128)} collective-permute-done((f32[3,32,64,24]{2,3,1,0:T(8,128)}, f32[3,32,64,24]{2,3,1,0:T(8,128)}, u32[]{:S(2)}, u32[]{:S(2)}) %collective-permute-start.2) | collective-permute-done | bytes 589856 | tf_op jit(solution)/shard_map/ppermute | solution.py:19
  55.3 3.3 %copy.36 = f32[3,32,64,24]{3,2,1,0:T(8,128)} copy(f32[3,32,64,24]{2,3,1,0:T(8,128)} %collective-permute-done.2) | data formatting | bytes 1179648 | tf_op jit(solution)/shard_map/ppermute | solution.py:19
  58.6 4.8 %collective-permute-done.3 = f32[3,32,64,24]{2,3,1,0:T(8,128)} collective-permute-done((f32[3,32,64,24]{2,3,1,0:T(8,128)}, f32[3,32,64,24]{2,3,1,0:T(8,128)}, u32[]{:S(2)}, u32[]{:S(2)}) %collective-permute-start.3) | collective-permute-done | bytes 589856 | tf_op jit(solution)/shard_map/ppermute | solution.py:22
  63.3 3.2 %copy.37 = f32[3,32,64,24]{3,2,1,0:T(8,128)} copy(f32[3,32,64,24]{2,3,1,0:T(8,128)} %collective-permute-done.3) | data formatting | bytes 1179648 | tf_op jit(solution)/shard_map/ppermute | solution.py:22
  66.5 9.4 %fusion = f32[3,32,64,128]{3,2,1,0:T(8,128)S(1)} fusion(f32[3,32,64,24]{3,2,1,0:T(8,128)} %copy.37, f32[3,32,64,128]{3,2,1,0:T(8,128)S(1)} %fusion.12, f32[3,32,64,24]{3,2,1,0:T(8,128)} %copy.36, f32[3]{0:T(128)S(1)} %sqrt.15, f32[3]{0:T(128)S(1)} %get-tuple-element.20, f32[128,176]{0,1:T(8,128)S(1)} %multiply_multiply_fusion, pred[128,176]{0,1:T(8,128)(4,1)S(1)} %fusion.38), kind=kOutput, calls=%fused_computation.1 | convolution fusion | flops 1663309824 | bytes 7583768 | tf_op jit(solution)/shard_map/ctyk,czk->ctyz/dot_general | solution.py:50
  77.4 2.0 %copy.38 = bf16[1,32,64,128]{1,3,2,0:T(8,128)(2,1)S(1)} copy(bf16[1,32,64,128]{3,2,1,0:T(8,128)(2,1)} %get-tuple-element.7) | data formatting | bytes 1048576 | tf_op jit(solution)/shard_map/convert.5
  79.4 1.9 %copy.39 = bf16[1,32,64,128]{1,3,2,0:T(8,128)(2,1)} copy(bf16[1,32,64,128]{3,2,1,0:T(8,128)(2,1)S(1)} %get-tuple-element.9) | data formatting | bytes 1048576 | tf_op jit(solution)/shard_map/convert.4
  81.3 1.9 %copy.40 = bf16[1,32,64,128]{1,3,2,0:T(8,128)(2,1)} copy(bf16[1,32,64,128]{3,2,1,0:T(8,128)(2,1)S(1)} %get-tuple-element.8) | data formatting | bytes 1048576 | tf_op jit(solution)/shard_map/convert.3
  83.1 9.5 %maximum_bitcast_fusion = bf16[16,32,3,32,4,4]{3,5,1,4,0,2:T(4,128)(2,1)} fusion(bf16[1,32,16,4,32,4]{1,5,4,3,2,0:T(4,128)(2,1)} %bitcast.55, bf16[1,32,16,4,32,4]{1,5,4,3,2,0:T(4,128)(2,1)} %bitcast.54, bf16[1,32,16,4,32,4]{1,5,4,3,2,0:T(4,128)(2,1)S(1)} %bitcast.53), kind=kLoop, calls=%fused_computation.7 | loop fusion | flops 1572864 | bytes 3145728 | tf_op jit(solution)/shard_map/transpose | solution.py:67
  92.6 14.5 %copy.41 = bf16[16,32,3,32,4,4]{1,0,5,4,3,2:T(8,128)(2,1)} copy(bf16[16,32,3,32,4,4]{3,5,1,4,0,2:T(4,128)(2,1)} %maximum_bitcast_fusion) | data formatting | bytes 3145728 | tf_op jit(solution)/shard_map/transpose | solution.py:67
  107.1 8.4 %reshape.178 = bf16[512,1536]{0,1:T(8,128)(2,1)S(1)} reshape(bf16[16,32,3,32,4,4]{1,0,5,4,3,2:T(8,128)(2,1)} %copy.41) | data formatting | bytes 3145728 | tf_op jit(solution)/shard_map/reshape | solution.py:67
  115.4 1.6 copy.42
  117.0 5.1 %scatter_custom_fusion = bf16[1024,1536]{1,0:T(8,128)(2,1)S(1)} fusion(s32[512]{0:T(512)S(1)} %bitcast.59, bf16[512,1536]{1,0:T(8,128)(2,1)} %copy.42, bf16[]{:T(256)} %constant.11.clone.1), kind=kCustom, calls=%fused_computation.15 | custom fusion | bytes 3146240 | tf_op jit(solution)/shard_map/scatter | solution.py:77
  122.1 54.2 %all_to_all.5 = bf16[128,8,1536]{2,1,0:T(8,128)(2,1)S(1)} all-to-all(bf16[128,8,1536]{2,1,0:T(8,128)(2,1)S(1)} %bitcast.51), channel_id=1, replica_groups=mesh['span'=16,'wall'=8] {'span','wall'}, dimensions={0} | all-to-all | bytes 6291456 | tf_op jit(solution)/shard_map/all_to_all | solution.py:78
  176.3 1.7 copy.46
  (32 shorter events, 5.9 us)
Async XLA Ops:
  1.5 15.9 %collective-permute-start = (bf16[3,32,24,128]{3,2,1,0:T(8,128)(2,1)S(1)}, bf16[3,32,24,128]{3,2,1,0:T(8,128)(2,1)S(1)}, u32[]{:S(2)}, u32[]{:S(2)}) collective-permute-start(bf16[3,32,24,128]{3,2,1,0:T(8,128)(2,1)S(1)} %get-tuple-element.12), channel_id=1, source_target_pairs={{0,1},{1,2},{2,3},{3,4},{4,5},{5,6},{6,7},{8,9},{9,10},{10,11},{11... | collective-permute-start | bytes 1769480 | tf_op jit(solution)/shard_map/ppermute | solution.py:19
  5.5 15.8 %collective-permute-start.1 = (bf16[3,32,24,128]{3,2,1,0:T(8,128)(2,1)S(1)}, bf16[3,32,24,128]{3,2,1,0:T(8,128)(2,1)S(1)}, u32[]{:S(2)}, u32[]{:S(2)}) collective-permute-start(bf16[3,32,24,128]{3,2,1,0:T(8,128)(2,1)S(1)} %get-tuple-element.13), channel_id=1, source_target_pairs={{1,0},{2,1},{3,2},{4,3},{5,4},{6,5},{7,6},{9,8},{10,9},{11,10},{12... | collective-permute-start | bytes 1769480 | tf_op jit(solution)/shard_map/ppermute | solution.py:22
  17.4 3.8 %copy-start.3 = (bf16[3,32,24,128]{3,2,1,0:T(8,128)(2,1)}, bf16[3,32,24,128]{3,2,1,0:T(8,128)(2,1)S(1)}, u32[]{:S(2)}) copy-start(bf16[3,32,24,128]{3,2,1,0:T(8,128)(2,1)S(1)} %collective-permute-done) | copy-start | bytes 1769476
  21.2 0.8 copy-start.4
  32.2 6.3 %copy-start = (s32[1,1,512,1]{2,3,1,0:T(1,128)S(1)}, s32[1,1,512,1]{2,3,1,0:T(1,128)}, u32[]{:S(2)}) copy-start(s32[1,1,512,1]{2,3,1,0:T(1,128)} %param.11) | copy-start | bytes 6148
  32.2 6.5 %copy-start.1 = (f32[6,64]{1,0:T(8,128)S(1)}, f32[6,64]{1,0:T(8,128)}, u32[]{:S(2)}) copy-start(f32[6,64]{1,0:T(8,128)} %param.9) | copy-start | bytes 4612
  32.2 23.1 %collective-permute-start.2 = (f32[3,32,64,24]{2,3,1,0:T(8,128)}, f32[3,32,64,24]{2,3,1,0:T(8,128)}, u32[]{:S(2)}, u32[]{:S(2)}) collective-permute-start(f32[3,32,64,24]{2,3,1,0:T(8,128)} %copy.34), channel_id=1, source_target_pairs={{0,8},{8,16},{16,24},{24,32},{32,40},{40,48},{48,56},{56,64},{64,7... | collective-permute-start | bytes 1769480 | tf_op jit(solution)/shard_map/ppermute | solution.py:19
  38.4 24.9 %collective-permute-start.3 = (f32[3,32,64,24]{2,3,1,0:T(8,128)}, f32[3,32,64,24]{2,3,1,0:T(8,128)}, u32[]{:S(2)}, u32[]{:S(2)}) collective-permute-start(f32[3,32,64,24]{2,3,1,0:T(8,128)} %copy.35), channel_id=1, source_target_pairs={{8,0},{16,8},{24,16},{32,24},{40,32},{48,40},{56,48},{64,56},{72,6... | collective-permute-start | bytes 1769480 | tf_op jit(solution)/shard_map/ppermute | solution.py:22
  66.5 9.4 %copy-start.2 = (f32[64]{0:T(128)S(1)}, f32[64]{0:T(128)}, u32[]{:S(2)}) copy-start(f32[64]{0:T(128)} %param.10) | copy-start | bytes 772
where the time goes:
time: 179 us; the launch traced here: 178 us
  local copies, waits for them, and re-layouts  56.7 us (32%)
  blocking collectives  54.2 us (30%)
  waiting for transfers between devices  33.6 us (19%)
  matrix products  12.6 us (7%)
  other arithmetic  12.4 us (7%)
  starting transfers between devices  8.32 us (5%)
    all_to_all x1, blocking collectives, per_device(): lax.all_to_all(outgoing.reshape(devices, slots, payload.shape[1]), ('span...  54.2 us
    ppermute x2, waiting for transfers between devices, with_halo(): lax.ppermute(lax.slice_in_dim(block, block.shape[dim] - width, None, axis...  25 us
    transpose x1, local copies, waits for them, and re-layouts, per_device(): jnp.transpose(blocks, (2, 4, 0, 1, 3, 5))  14.5 us
    reshape x2, local copies, waits for them, and re-layouts, per_device(): jnp.transpose(blocks, (2, 4, 0, 1, 3, 5))  9.94 us
    transpose x1, other arithmetic, per_device(): jnp.transpose(blocks, (2, 4, 0, 1, 3, 5))  9.46 us
    dot_general x1, matrix products, span_pass(): jnp.einsum('ctyk,czk->ctyz', extended, matrix, precision=lax.Precision.HI...  9.42 us
    ppermute x2, waiting for transfers between devices, with_halo(): lax.ppermute(lax.slice_in_dim(block, 0, width, axis=dim), axis, backward)  8.59 us
    slice x3, local copies, waits for them, and re-layouts, with_halo(): lax.slice_in_dim(block, block.shape[dim] - width, None, axis=dim)  8.45 us
  transfers between devices with their start and end apart: 4, of which 4 were waited for; matrix products, arithmetic and copies ran while one was open for 5% of the time, Pallas kernels for 0%

commit v1 on v0

v1 whole, which is shorter than its diff:
```python
import functools
import math

import jax
import jax.numpy as jnp
from jax import lax
from jax.experimental import pallas as pl
from jax.experimental.pallas import tpu as pltpu
from jax.sharding import PartitionSpec as P

HALO = 24
EDGE = 4
F32 = jnp.float32
BF16 = jnp.bfloat16


def iota(shape, dim):
    return lax.broadcasted_iota(jnp.int32, shape, dim)


def split(x):
    hi = x.astype(BF16)
    return hi, (x - hi.astype(F32)).astype(BF16)


def dot(a, b):
    return jnp.dot(a, b, preferred_element_type=F32)


def dot_nt(a, b):
    return lax.dot_general(a, b, (((1,), (1,)), ((), ())), preferred_element_type=F32)


def tap_coefficients(scale):
    square = jnp.full((1, 128), scale, F32)
    square = square * square
    lane = iota((1, 128), 1)
    k = (lane - HALO).astype(F32)
    energy = jnp.where(lane <= 2 * HALO, jnp.exp(-math.pi * k * k / square), 0.0)
    norm = jnp.sqrt(jnp.sum(energy, axis=1, keepdims=True))
    return (math.pi / (2.0 * square))[:, :1], 1.0 / norm


def tap_values(offset, valid, coefficients):
    rate, gain = coefficients
    d = offset.astype(F32)
    inside = valid & (offset >= -HALO) & (offset <= HALO)
    return jnp.where(inside, jnp.exp(-(d * d) * rate) * gain, 0.0)


def wall_operand(scale, wall, n_wall):
    shape = (128, 224)
    r, k = iota(shape, 0), iota(shape, 1)
    y = EDGE * (r >> 3) + (r & 3)
    t = (r >> 2) & 1
    core, low = k < 128, k < 176
    j = jnp.where(low, k - 128, k - 176)
    t_halo = (j >= HALO).astype(jnp.int32)
    inner = j - HALO * t_halo
    t_col = jnp.where(core, k >> 6, t_halo)
    y_col = jnp.where(core, k & 63, jnp.where(low, inner - HALO, inner + 64))
    first = (wall > 0).astype(jnp.int32)
    last = (wall < n_wall - 1).astype(jnp.int32)
    present = jnp.where(core, 1, jnp.where(low, first, last)) > 0
    values = tap_values(y_col - y, (t == t_col) & present, tap_coefficients(scale))
    hi, lo = split(values)
    return jnp.concatenate([hi, lo], axis=0)


def span_operands(scale):
    coefficients = tap_coefficients(scale)
    shape = (128, 128)
    r, k = iota(shape, 0), iota(shape, 1)
    z = EDGE * (r & 31) + (r >> 5)
    hi, lo = split(tap_values(k - z, r >= 0, coefficients))
    row, col = iota((96, 256), 0), iota((96, 256), 1)
    g = (row >= 24).astype(jnp.int32) + (row >= 48).astype(jnp.int32) + (row >= 72).astype(jnp.int32)
    inner = row - HALO * g
    source = inner + jnp.where(g < 2, 128 - HALO, 0) + 128 * (g & 1)
    pick = jnp.where(col == source, 1.0, 0.0).astype(BF16)
    own = jnp.concatenate(
        [
            jnp.concatenate([hi, hi], axis=1),
            jnp.concatenate([lo, jnp.zeros_like(lo)], axis=1),
            pick,
        ],
        axis=0,
    )
    shape = (128, 192)
    r, k = iota(shape, 0), iota(shape, 1)
    z = EDGE * (r & 31) + (r >> 5)
    second = k >= 96
    j = jnp.where(second, k - 96, k)
    right = j >= 48
    j = jnp.where(right, j - 48, j)
    low_term = j >= HALO
    j = jnp.where(low_term, j - HALO, j)
    column = jnp.where(right, 128 + j, j - HALO)
    values = tap_values(column - z, r >= 0, coefficients)
    hi = values.astype(BF16).astype(F32)
    strips = jnp.where(second, jnp.where(low_term, 0.0, values - hi), hi).astype(BF16)
    return own, strips


def wall_pass(c, noise_ref, low_ref, high_ref, operand, smooth_ref):
    planes = noise_ref.shape[1]
    for q in range(planes // 4):
        blocks = []
        for p in (2 * q, 2 * q + 1):
            at = (c * planes // 2 + p) * 2 * HALO
            blocks.append(
                jnp.concatenate(
                    [
                        noise_ref[c, 2 * p : 2 * p + 2].reshape(128, 128),
                        low_ref[at : at + 2 * HALO],
                        high_ref[at : at + 2 * HALO],
                    ],
                    axis=0,
                )
            )
        both = dot(operand, jnp.concatenate(blocks, axis=1))
        both = both[:128] + both[128:]
        smooth_ref[:, 2 * q] = both[:, :128].reshape(16, 8, 128)
        smooth_ref[:, 2 * q + 1] = both[:, 128:].reshape(16, 8, 128)


def front_kernel(n_wall, wscale, sscale, noise_ref, low_ref, high_ref, centre_ref, to_next_ref, to_prev_ref, smooth_ref):
    wall = lax.axis_index("wall")
    for c in range(3):
        wall_pass(c, noise_ref, low_ref, high_ref, wall_operand(wscale[c], wall, n_wall), smooth_ref)
        own, _ = span_operands(sscale[c])
        for g in range(8):
            hi, lo = split(smooth_ref[2 * g : 2 * g + 2].reshape(256, 128))
            out = dot_nt(own, jnp.concatenate([hi, lo], axis=1))
            lanes = slice(256 * g, 256 * g + 256)
            centre_ref[c, :, lanes] = out[:128] + out[128:256]
            to_next_ref[c, :, lanes] = out[256:304].astype(BF16)
            to_prev_ref[c, :, lanes] = out[304:352].astype(BF16)


def lane_factors(fac):
    first, rest = fac.astype(BF16), None
    rest = fac - first.astype(F32)
    second = rest.astype(BF16)
    third = (rest - second.astype(F32)).astype(BF16)
    lane = iota((64, 2048), 1)
    spread = jnp.where(iota((64, 2048), 0) == EDGE * (lane >> 7) + (lane & 3), 1.0, 0.0).astype(BF16)
    return dot(first, spread) + dot(second, spread) + dot(third, spread)


def slot_onehot(owner, devices, slots):
    n = owner.shape[1]
    mine = jnp.where(iota((devices, n), 0) == owner, 1.0, 0.0)
    before = jnp.where(iota((n, n), 0) < iota((n, n), 1), 1.0, 0.0).astype(BF16)
    count = dot(mine.astype(BF16), before)
    rank = jnp.sum(mine * count, axis=0, keepdims=True).astype(jnp.int32)
    target = owner * slots + rank
    return jnp.where(iota((devices * slots, n), 0) == target, 1.0, 0.0).astype(BF16)


def interleave_matrix():
    k, n = iota((512, 512), 0), iota((512, 512), 1)
    return jnp.where(n == EDGE * (k & 127) + (k >> 7), 1.0, 0.0).astype(BF16)


def velocity_of(c, psi, fac_ref, lanes):
    def f(i):
        return fac_ref[i : i + 1, lanes]

    if c == 0:
        return f(6) + f(0) * psi[0]
    if c == 1:
        return f(1) * psi[0] + f(2) * psi[1]
    return f(3) * psi[0] + f(4) * psi[1] + f(5) * psi[2]


def back_kernel(devices, slots, sscale, centre_ref, left_ref, right_ref, fac_ref, owner_ref, out_ref, psi_ref, lanes_ref, hot_ref, tile_ref):
    lanes_ref[...] = lane_factors(fac_ref[...])
    hot_ref[...] = slot_onehot(owner_ref[...], devices, slots)
    interleave = interleave_matrix()
    for c in range(3):
        _, strips = span_operands(sscale[c])
        for g in range(8):
            lanes = slice(256 * g, 256 * g + 256)
            left, right = left_ref[c, :, lanes], right_ref[c, :, lanes]
            psi_c = centre_ref[c, :, lanes] + dot(strips, jnp.concatenate([left, right, left, right], axis=0))
            if c < 2:
                psi_ref[c, :, lanes] = psi_c
            psi = [psi_ref[i, :, lanes] for i in range(c)] + [psi_c]
            velocity = velocity_of(c, psi, lanes_ref, lanes).astype(BF16)
            for e in range(2):
                for dz in range(EDGE):
                    tile_ref[32 * (2 * g + e) : 32 * (2 * g + e) + 32, 128 * dz : 128 * dz + 128] = velocity[
                        32 * dz : 32 * dz + 32, 128 * e : 128 * e + 128
                    ]
        payload = dot(tile_ref[...], interleave).astype(BF16)
        for b in range(4):
            rows = slice(256 * b, 256 * b + 256)
            out_ref[rows, 512 * c : 512 * c + 512] = dot(hot_ref[rows], payload).astype(BF16)


VMEM = pl.BlockSpec(memory_space=pltpu.VMEM)
SMEM = pl.BlockSpec(memory_space=pltpu.SMEM)


def front(noise, low, high, wall_scale, span_scale, n_wall):
    return pl.pallas_call(
        functools.partial(front_kernel, n_wall),
        out_shape=(
            jax.ShapeDtypeStruct((3, 128, 2048), F32),
            jax.ShapeDtypeStruct((3, 48, 2048), BF16),
            jax.ShapeDtypeStruct((3, 48, 2048), BF16),
        ),
        in_specs=[SMEM, SMEM, VMEM, VMEM, VMEM],
        out_specs=(VMEM, VMEM, VMEM),
        scratch_shapes=[pltpu.VMEM((16, 16, 8, 128), F32)],
        name="front",
    )(wall_scale, span_scale, noise, low, high)


def back(centre, left, right, fac, owner, span_scale, devices, slots):
    return pl.pallas_call(
        functools.partial(back_kernel, devices, slots),
        out_shape=jax.ShapeDtypeStruct((devices * slots, 1536), BF16),
        in_specs=[SMEM, VMEM, VMEM, VMEM, VMEM, VMEM],
        out_specs=VMEM,
        scratch_shapes=[
            pltpu.VMEM((2, 128, 2048), F32),
            pltpu.VMEM((8, 2048), F32),
            pltpu.VMEM((devices * slots, 512), BF16),
            pltpu.VMEM((512, 512), BF16),
        ],
        name="back",
    )(span_scale, centre, left, right, fac, owner)


def per_device(noise, wall_scale, span_scale, lund_factor, mean_velocity, owner_map):
    planes, rows = noise.shape[1:3]
    n_span, n_wall = lax.axis_size("span"), lax.axis_size("wall")
    devices = n_span * n_wall
    slots = 8
    up = [(i, (i + 1) % n_wall) for i in range(n_wall)]
    down = [(b, a) for a, b in up]
    low = lax.ppermute(noise[:, :, rows - HALO :], "wall", up)
    high = lax.ppermute(noise[:, :, :HALO], "wall", down)
    fac = jnp.concatenate([lund_factor, mean_velocity[None], jnp.zeros((1, rows), F32)], axis=0)
    centre, to_next, to_prev = front(
        noise, low.reshape(-1, 128), high.reshape(-1, 128), wall_scale, span_scale, n_wall
    )
    ahead = [(i, (i + 1) % n_span) for i in range(n_span)]
    left = lax.ppermute(to_next, "span", ahead)
    right = lax.ppermute(to_prev, "span", [(b, a) for a, b in ahead])
    outgoing = back(centre, left, right, fac, owner_map.reshape(1, -1), span_scale, devices, slots)
    received = lax.all_to_all(
        outgoing.reshape(devices, slots, -1), ("span", "wall"), split_axis=0, concat_axis=0, tiled=True
    )
    return received.reshape(1, devices * slots, -1)


def solution(mesh):
    return jax.shard_map(
        per_device,
        mesh=mesh,
        in_specs=(
            P(None, None, "wall", "span"),
            P(),
            P(),
            P(None, "wall"),
            P("wall"),
            P("wall", "span", None, None),
        ),
        out_specs=P(("span", "wall"), None, None),
        check_vma=False,
    )
```

time: 179 us -> 108 us (0.60)
  local copies, waits for them, and re-layouts: 56.7 us -> 4.89 us
  Pallas kernels: 0 us -> 14.4 us
  matrix products: 12.6 us -> 0 us
  other arithmetic: 12.4 us -> 0.65 us
  blocking collectives: 54.2 us -> 47.5 us
    transpose x1 -> x0, local copies, waits for them, and re-layouts: 14.5 us -> none  [per_device(): jnp.transpose(blocks, (2, 4, 0, 1, 3, 5))]
    pallas_call x0 -> x2, Pallas kernels: none -> 14.4 us  [the longest x1 7.98 us: back(): pl.pallas_call(functools.partial(back_kernel, devices, slots), out_shape=...]
    dot_general x2 -> x0, matrix products: 12.6 us -> none  [the longest x1 9.42 us: span_pass(): jnp.einsum('ctyk,czk->ctyz', extended, matrix, precision=lax.Precision.HI...]
    slice x4 -> x1, local copies, waits for them, and re-layouts: 11.6 us -> 1.49 us  [per_device(): high = lax.ppermute(noise[:, :, :HALO], 'wall', down)]
    reshape x2 -> x0, local copies, waits for them, and re-layouts: 9.94 us -> none  [per_device(): jnp.transpose(blocks, (2, 4, 0, 1, 3, 5))]
    transpose x1 -> x0, other arithmetic: 9.46 us -> none  [per_device(): jnp.transpose(blocks, (2, 4, 0, 1, 3, 5))]
    all_to_all x1, blocking collectives: 54.2 us -> 47.5 us  [per_device(): lax.all_to_all(outgoing.reshape(devices, slots, -1), ('span', 'wall'), sp...]
    ppermute x2 -> x0, local copies, waits for them, and re-layouts: 6.5 us -> none  [the longest x1 3.28 us: with_halo(): lax.ppermute(lax.slice_in_dim(block, block.shape[dim] - width, None, axis...]
  transfers between devices with their start and end apart: 4 -> 4, of which waited for: 4 -> 4; matrix products, arithmetic and copies ran while one was open for 5% -> 1% of each run, Pallas kernels for 0% -> 0%
where the time goes in v1:
time: 108 us
  blocking collectives  47.5 us (44%)
  waiting for transfers between devices  32.3 us (30%)
  Pallas kernels  14.4 us (13%)
  starting transfers between devices  8.15 us (8%)
  local copies, waits for them, and re-layouts  4.89 us (5%)
    all_to_all x1, blocking collectives, per_device(): lax.all_to_all(outgoing.reshape(devices, slots, -1), ('span', 'wall'), sp...  47.5 us
    ppermute x1, waiting for transfers between devices, per_device(): high = lax.ppermute(noise[:, :, :HALO], 'wall', down)  12 us
    ppermute x1, waiting for transfers between devices, per_device(): left = lax.ppermute(to_next, 'span', ahead)  8.89 us
    pallas_call x1, Pallas kernels, back(): pl.pallas_call(functools.partial(back_kernel, devices, slots), out_shape=...  7.98 us
    pallas_call x1, Pallas kernels, front(): pl.pallas_call(functools.partial(front_kernel, n_wall), out_shape=(jax.Sh...  6.4 us
    ppermute x1, starting transfers between devices, per_device(): high = lax.ppermute(noise[:, :, :HALO], 'wall', down)  6.01 us
    ppermute x1, waiting for transfers between devices, per_device(): right = lax.ppermute(to_prev, 'span', [(b, a) for a, b in ahead])  5.91 us
    ppermute x1, waiting for transfers between devices, per_device(): low = lax.ppermute(noise[:, :, rows - HALO:], 'wall', up)  5.49 us
  transfers between devices with their start and end apart: 4, of which 4 were waited for; matrix products, arithmetic and copies ran while one was open for 1% of the time, Pallas kernels for 0%

profile of v1, /device:TPU:1, one launch (start us, length us, event | category | flops | bytes accessed | tf_op | source)
XLA Modules:
  0.0 107.9 jit_solution(17042168338836116945)
XLA Ops:
  0.0 0.0 copy-start.5
  0.0 0.0 copy-start.4
  0.0 1.5 %fusion = (bf16[3,32,24,128]{3,2,1,0:T(8,128)(2,1)S(1)}, bf16[3,32,24,128]{3,2,1,0:T(8,128)(2,1)S(1)}) fusion(bf16[3,32,64,128]{3,2,1,0:T(8,128)(2,1)} %noise_ref.1), kind=kLoop, calls=%fused_computation.1 | loop fusion | bytes 2359296 | tf_op jit(solution)/shard_map/slice | solution.py:245
  1.5 6.0 %collective-permute-start.1 = (bf16[3,32,24,128]{3,2,1,0:T(8,128)(2,1)S(1)}, bf16[3,32,24,128]{3,2,1,0:T(8,128)(2,1)S(1)}, u32[]{:S(2)}, u32[]{:S(2)}) collective-permute-start(bf16[3,32,24,128]{3,2,1,0:T(8,128)(2,1)S(1)} %get-tuple-element.11), channel_id=1, source_target_pairs={{1,0},{2,1},{3,2},{4,3},{5,4},{6,5},{7,6},{0,7},{9,8},{10,9},{11,1... | collective-permute-start | bytes 1769480 | tf_op jit(solution)/shard_map/ppermute | solution.py:245
  7.5 0.0 collective-permute-start
  7.5 12.0 %collective-permute-done.1 = bf16[3,32,24,128]{3,2,1,0:T(8,128)(2,1)S(1)} collective-permute-done((bf16[3,32,24,128]{3,2,1,0:T(8,128)(2,1)S(1)}, bf16[3,32,24,128]{3,2,1,0:T(8,128)(2,1)S(1)}, u32[]{:S(2)}, u32[]{:S(2)}) %collective-permute-start.1) | collective-permute-done | bytes 589856 | tf_op jit(solution)/shard_map/ppermute | solution.py:245
  19.5 0.0 copy-start
  19.5 5.5 %collective-permute-done = bf16[3,32,24,128]{3,2,1,0:T(8,128)(2,1)S(1)} collective-permute-done((bf16[3,32,24,128]{3,2,1,0:T(8,128)(2,1)S(1)}, bf16[3,32,24,128]{3,2,1,0:T(8,128)(2,1)S(1)}, u32[]{:S(2)}, u32[]{:S(2)}) %collective-permute-start) | collective-permute-done | bytes 589856 | tf_op jit(solution)/shard_map/ppermute | solution.py:244
  25.0 0.0 copy-done
  25.0 0.8 copy-done.1
  25.8 6.4 %front.1 = (f32[3,128,2048]{2,1,0:T(8,128)}, bf16[3,48,2048]{2,1,0:T(8,128)(2,1)}, bf16[3,48,2048]{2,1,0:T(8,128)(2,1)}) custom-call(f32[3]{0:T(128)} %wscale.1, f32[3]{0:T(128)} %sscale.3, bf16[3,32,64,128]{3,2,1,0:T(8,128)(2,1)} %noise_ref.1, bf16[2304,128]{1,0:T(8,128)(2,1)} %bitcast.10, bf16[2304,128]{1,0:T(8,128)(2,1)} %bitcast.9), custom_call_target="tpu_custom_call" | custom-call | tf_op jit(solution)/shard_map/front/pallas_call | solution.py:207
  32.2 2.1 %collective-permute-start.2 = (bf16[3,48,2048]{2,1,0:T(8,128)(2,1)}, bf16[3,48,2048]{2,1,0:T(8,128)(2,1)S(1)}, u32[]{:S(2)}, u32[]{:S(2)}) collective-permute-start(bf16[3,48,2048]{2,1,0:T(8,128)(2,1)} %get-tuple-element.9), channel_id=1, source_target_pairs={{0,8},{8,16},{16,24},{24,32},{32,40},{40,48},{48,56},{56,64},{64,7... | collective-permute-start | bytes 1769480 | tf_op jit(solution)/shard_map/ppermute | solution.py:251
  34.4 0.0 collective-permute-start.3
  34.4 0.1 pad.2.clone
  34.5 0.0 copy-done.5
  34.5 0.0 copy-done.4
  34.5 0.7 maximum_maximum_fusion.fac_ref
  35.1 8.9 %collective-permute-done.2.left_ref = bf16[3,48,2048]{2,1,0:T(8,128)(2,1)S(1)} collective-permute-done((bf16[3,48,2048]{2,1,0:T(8,128)(2,1)}, bf16[3,48,2048]{2,1,0:T(8,128)(2,1)S(1)}, u32[]{:S(2)}, u32[]{:S(2)}) %collective-permute-start.2) | collective-permute-done | bytes 589856 | tf_op jit(solution)/shard_map/ppermute | solution.py:251
  44.0 5.9 %collective-permute-done.3.right_ref = bf16[3,48,2048]{2,1,0:T(8,128)(2,1)S(1)} collective-permute-done((bf16[3,48,2048]{2,1,0:T(8,128)(2,1)}, bf16[3,48,2048]{2,1,0:T(8,128)(2,1)S(1)}, u32[]{:S(2)}, u32[]{:S(2)}) %collective-permute-start.3) | collective-permute-done | bytes 589856 | tf_op jit(solution)/shard_map/ppermute | solution.py:252
  49.9 0.0 copy-done.2
  49.9 0.8 copy-done.3
  50.7 8.0 %back.1 = bf16[1024,1536]{1,0:T(8,128)(2,1)} custom-call(f32[3]{0:T(128)} %sscale.3, f32[3,128,2048]{2,1,0:T(8,128)} %get-tuple-element.8.centre_ref, bf16[3,48,2048]{2,1,0:T(8,128)(2,1)} %copy-done.2, bf16[3,48,2048]{2,1,0:T(8,128)(2,1)} %copy-done.3, f32[8,64]{1,0:T(8,128)} %maximum_maximum_fusion.fac_ref, s32[1,512]{1,0:T(1,128)} %bitcast.11), custom_call_target="tpu_custom_call" | custom-call | tf_op jit(solution)/shard_map/back/pallas_call | solution.py:222
  58.7 47.5 %all_to_all.5 = bf16[128,8,1536]{2,1,0:T(8,128)(2,1)S(1)} all-to-all(bf16[128,8,1536]{2,1,0:T(8,128)(2,1)} %bitcast.8), channel_id=1, replica_groups=mesh['span'=16,'wall'=8] {'span','wall'}, dimensions={0} | all-to-all | bytes 6291456 | tf_op jit(solution)/shard_map/all_to_all | solution.py:254
  106.2 1.7 %copy.8 = bf16[1,1024,1536]{2,1,0:T(8,128)(2,1)} copy(bf16[1,1024,1536]{2,1,0:T(8,128)(2,1)S(1)} %bitcast.7) | data formatting | bytes 6291456
  (3 shorter events, 0.0 us)
Async XLA Ops:
  0.0 34.5 %copy-start.5 = (f32[64]{0:T(128)S(1)}, f32[64]{0:T(128)}, u32[]{:S(2)}) copy-start(f32[64]{0:T(128)} %param.10) | copy-start | bytes 772
  0.0 34.5 %copy-start.4 = (f32[6,64]{1,0:T(8,128)S(1)}, f32[6,64]{1,0:T(8,128)}, u32[]{:S(2)}) copy-start(f32[6,64]{1,0:T(8,128)} %param.9) | copy-start | bytes 4612
  1.5 18.0 %collective-permute-start.1 = (bf16[3,32,24,128]{3,2,1,0:T(8,128)(2,1)S(1)}, bf16[3,32,24,128]{3,2,1,0:T(8,128)(2,1)S(1)}, u32[]{:S(2)}, u32[]{:S(2)}) collective-permute-start(bf16[3,32,24,128]{3,2,1,0:T(8,128)(2,1)S(1)} %get-tuple-element.11), channel_id=1, source_target_pairs={{1,0},{2,1},{3,2},{4,3},{5,4},{6,5},{7,6},{0,7},{9,8},{10,9},{11,1... | collective-permute-start | bytes 1769480 | tf_op jit(solution)/shard_map/ppermute | solution.py:245
  7.5 17.5 %collective-permute-start = (bf16[3,32,24,128]{3,2,1,0:T(8,128)(2,1)S(1)}, bf16[3,32,24,128]{3,2,1,0:T(8,128)(2,1)S(1)}, u32[]{:S(2)}, u32[]{:S(2)}) collective-permute-start(bf16[3,32,24,128]{3,2,1,0:T(8,128)(2,1)S(1)} %get-tuple-element.12), channel_id=1, source_target_pairs={{0,1},{1,2},{2,3},{3,4},{4,5},{5,6},{6,7},{7,0},{8,9},{9,10},{10,1... | collective-permute-start | bytes 1769480 | tf_op jit(solution)/shard_map/ppermute | solution.py:244
  19.5 5.5 %copy-start = (bf16[3,32,24,128]{3,2,1,0:T(8,128)(2,1)}, bf16[3,32,24,128]{3,2,1,0:T(8,128)(2,1)S(1)}, u32[]{:S(2)}) copy-start(bf16[3,32,24,128]{3,2,1,0:T(8,128)(2,1)S(1)} %collective-permute-done.1) | copy-start | bytes 1769476
  25.0 0.8 copy-start.1
  32.2 11.8 %collective-permute-start.2 = (bf16[3,48,2048]{2,1,0:T(8,128)(2,1)}, bf16[3,48,2048]{2,1,0:T(8,128)(2,1)S(1)}, u32[]{:S(2)}, u32[]{:S(2)}) collective-permute-start(bf16[3,48,2048]{2,1,0:T(8,128)(2,1)} %get-tuple-element.9), channel_id=1, source_target_pairs={{0,8},{8,16},{16,24},{24,32},{32,40},{40,48},{48,56},{56,64},{64,7... | collective-permute-start | bytes 1769480 | tf_op jit(solution)/shard_map/ppermute | solution.py:251
  34.4 15.5 %collective-permute-start.3 = (bf16[3,48,2048]{2,1,0:T(8,128)(2,1)}, bf16[3,48,2048]{2,1,0:T(8,128)(2,1)S(1)}, u32[]{:S(2)}, u32[]{:S(2)}) collective-permute-start(bf16[3,48,2048]{2,1,0:T(8,128)(2,1)} %get-tuple-element.10), channel_id=1, source_target_pairs={{8,0},{16,8},{24,16},{32,24},{40,32},{48,40},{56,48},{64,56},{72,6... | collective-permute-start | bytes 1769480 | tf_op jit(solution)/shard_map/ppermute | solution.py:252
  44.0 5.9 %copy-start.2 = (bf16[3,48,2048]{2,1,0:T(8,128)(2,1)}, bf16[3,48,2048]{2,1,0:T(8,128)(2,1)S(1)}, u32[]{:S(2)}) copy-start(bf16[3,48,2048]{2,1,0:T(8,128)(2,1)S(1)} %collective-permute-done.2.left_ref) | copy-start | bytes 1769476
  49.9 0.8 copy-start.3

commit v2 on v1

--- a/solution.py
+++ b/solution.py
@@ -107,13 +107,12 @@
     for q in range(planes // 4):
         blocks = []
         for p in (2 * q, 2 * q + 1):
-            at = (c * planes // 2 + p) * 2 * HALO
             blocks.append(
                 jnp.concatenate(
                     [
                         noise_ref[c, 2 * p : 2 * p + 2].reshape(128, 128),
-                        low_ref[at : at + 2 * HALO],
-                        high_ref[at : at + 2 * HALO],
+                        low_ref[c, 2 * p : 2 * p + 2].reshape(2 * HALO, 128),
+                        high_ref[c, 2 * p : 2 * p + 2].reshape(2 * HALO, 128),
                     ],
                     axis=0,
                 )
@@ -124,18 +123,14 @@
         smooth_ref[:, 2 * q + 1] = both[:, 128:].reshape(16, 8, 128)
 
 
-def front_kernel(n_wall, wscale, sscale, noise_ref, low_ref, high_ref, centre_ref, to_next_ref, to_prev_ref, smooth_ref):
-    wall = lax.axis_index("wall")
-    for c in range(3):
-        wall_pass(c, noise_ref, low_ref, high_ref, wall_operand(wscale[c], wall, n_wall), smooth_ref)
-        own, _ = span_operands(sscale[c])
-        for g in range(8):
-            hi, lo = split(smooth_ref[2 * g : 2 * g + 2].reshape(256, 128))
-            out = dot_nt(own, jnp.concatenate([hi, lo], axis=1))
-            lanes = slice(256 * g, 256 * g + 256)
-            centre_ref[c, :, lanes] = out[:128] + out[128:256]
-            to_next_ref[c, :, lanes] = out[256:304].astype(BF16)
-            to_prev_ref[c, :, lanes] = out[304:352].astype(BF16)
+def span_own_pass(c, own, smooth_ref, psi_ref, to_next_ref, to_prev_ref):
+    for g in range(8):
+        hi, lo = split(smooth_ref[2 * g : 2 * g + 2].reshape(256, 128))
+        out = dot_nt(own, jnp.concatenate([hi, lo], axis=1))
+        lanes = slice(256 * g, 256 * g + 256)
+        psi_ref[c, :, lanes] = out[:128] + out[128:256]
+        to_next_ref[c, :, lanes] = out[256:304].astype(BF16)
+        to_prev_ref[c, :, lanes] = out[304:352].astype(BF16)
 
 
 def lane_factors(fac):
@@ -174,85 +169,184 @@
     return f(3) * psi[0] + f(4) * psi[1] + f(5) * psi[2]
 
 
-def back_kernel(devices, slots, sscale, centre_ref, left_ref, right_ref, fac_ref, owner_ref, out_ref, psi_ref, lanes_ref, hot_ref, tile_ref):
+def finish(c, strips, left_ref, right_ref, psi_ref, lanes_ref, hot_ref, interleave_ref, tile_ref, outgoing_ref):
+    for g in range(8):
+        lanes = slice(256 * g, 256 * g + 256)
+        left, right = left_ref[c, :, lanes], right_ref[c, :, lanes]
+        psi_c = psi_ref[c, :, lanes] + dot(strips, jnp.concatenate([left, right, left, right], axis=0))
+        if c < 2:
+            psi_ref[c, :, lanes] = psi_c
+        psi = [psi_ref[i, :, lanes] for i in range(c)] + [psi_c]
+        velocity = velocity_of(c, psi, lanes_ref, lanes).astype(BF16)
+        for e in range(2):
+            for dz in range(EDGE):
+                tile_ref[32 * (2 * g + e) : 32 * (2 * g + e) + 32, 128 * dz : 128 * dz + 128] = velocity[
+                    32 * dz : 32 * dz + 32, 128 * e : 128 * e + 128
+                ]
+    payload = dot(tile_ref[...], interleave_ref[...]).astype(BF16)
+    for b in range(4):
+        part = dot(hot_ref[256 * b : 256 * b + 256], payload)
+        outgoing_ref[c, 32 * b : 32 * b + 32] = part.reshape(32, 8, 512).astype(BF16)
+
+
+def kernel(
+    n_span, n_wall, slots, wscale, sscale, noise_hbm, lund_ref, mean_ref, owner_ref, out_ref,
+    noise_ref, low_ref, high_ref, smooth_ref, psi_ref, to_next_ref, to_prev_ref, left_ref, right_ref,
+    fac_ref, lanes_ref, hot_ref, interleave_ref, tile_ref, outgoing_ref,
+    load_sem, halo_send, halo_recv, strip_send, strip_recv, out_send, out_recv, self_sem,
+):
+    devices = n_span * n_wall
+    span, wall = lax.axis_index("span"), lax.axis_index("wall")
+    me = span * n_wall + wall
+    rows = noise_hbm.shape[2]
+
+    def place(index):
+        return {"span": lax.div(index, n_wall), "wall": lax.rem(index, n_wall)}
+
+    barrier = pltpu.get_barrier_semaphore()
+
+    def greet(i, carry):
+        pl.semaphore_signal(barrier, inc=1, device_id=place(jnp.bitwise_xor(me, i)), device_id_type=MESH)
+        return carry
+
+    lax.fori_loop(1, devices, greet, 0)
+
+    loads = [pltpu.make_async_copy(noise_hbm.at[c], noise_ref.at[c], load_sem.at[c]) for c in range(3)]
+    for load in loads:
+        load.start()
+    fac_ref[...] = jnp.zeros_like(fac_ref)
+    fac_ref[0:6] = lund_ref[...]
+    fac_ref[6:7] = mean_ref[...]
     lanes_ref[...] = lane_factors(fac_ref[...])
     hot_ref[...] = slot_onehot(owner_ref[...], devices, slots)
-    interleave = interleave_matrix()
+    interleave_ref[...] = interleave_matrix()
+
+    def sends(c, step, size, axis, pairs, send_sem, recv_sem):
+        here = lax.axis_index(axis)
+        targets = (lax.rem(here + 1, size), lax.rem(here + size - 1, size))
+        return [
+            pltpu.make_async_remote_copy(
+                src_ref=src, dst_ref=dst, send_sem=send_sem.at[c, i], recv_sem=recv_sem.at[c, i],
+                device_id={axis: targets[i]}, device_id_type=MESH,
+            )
+            for i, (src, dst) in enumerate(pairs)
+        ]
+
+    halos = [
+        sends(
+            c, 0, n_wall, "wall",
+            (
+                (noise_hbm.at[c, :, pl.ds(rows - HALO, HALO), :], low_ref.at[c]),
+                (noise_hbm.at[c, :, pl.ds(0, HALO), :], high_ref.at[c]),
+            ),
+            halo_send, halo_recv,
+        )
+        for c in range(3)
+    ]
+    strips = [
+        sends(
+            c, 1, n_span, "span",
+            ((to_next_ref.at[c], left_ref.at[c]), (to_prev_ref.at[c], right_ref.at[c])),
+            strip_send, strip_recv,
+        )
+        for c in range(3)
+    ]
+
+    pl.semaphore_wait(barrier, devices - 1)
     for c in range(3):
-        _, strips = span_operands(sscale[c])
-        for g in range(8):
-            lanes = slice(256 * g, 256 * g + 256)
-            left, right = left_ref[c, :, lanes], right_ref[c, :, lanes]
-            psi_c = centre_ref[c, :, lanes] + dot(strips, jnp.concatenate([left, right, left, right], axis=0))
-            if c < 2:
-                psi_ref[c, :, lanes] = psi_c
-            psi = [psi_ref[i, :, lanes] for i in range(c)] + [psi_c]
-            velocity = velocity_of(c, psi, lanes_ref, lanes).astype(BF16)
-            for e in range(2):
-                for dz in range(EDGE):
-                    tile_ref[32 * (2 * g + e) : 32 * (2 * g + e) + 32, 128 * dz : 128 * dz + 128] = velocity[
-                        32 * dz : 32 * dz + 32, 128 * e : 128 * e + 128
-                    ]
-        payload = dot(tile_ref[...], interleave).astype(BF16)
-        for b in range(4):
-            rows = slice(256 * b, 256 * b + 256)
-            out_ref[rows, 512 * c : 512 * c + 512] = dot(hot_ref[rows], payload).astype(BF16)
+        for copy in halos[c]:
+            copy.start()
+
+    def early(c):
+        operand = wall_operand(wscale[c], wall, n_wall)
+        own, from_strips = span_operands(sscale[c])
+        loads[c].wait()
+        for copy in halos[c]:
+            copy.wait_recv()
+        wall_pass(c, noise_ref, low_ref, high_ref, operand, smooth_ref)
+        span_own_pass(c, own, smooth_ref, psi_ref, to_next_ref, to_prev_ref)
+        for copy in strips[c]:
+            copy.start()
+        return from_strips
+
+    def late(c, from_strips):
+        for copy in strips[c]:
+            copy.wait_recv()
+        finish(c, from_strips, left_ref, right_ref, psi_ref, lanes_ref, hot_ref, interleave_ref, tile_ref, outgoing_ref)
+        lanes = pl.ds(512 * c, 512)
+
+        def deliver(i, carry):
+            to = jnp.bitwise_xor(me, i)
+            pltpu.make_async_remote_copy(
+                src_ref=outgoing_ref.at[c, to], dst_ref=out_ref.at[me, :, lanes],
+                send_sem=out_send.at[c], recv_sem=out_recv.at[c], device_id=place(to), device_id_type=MESH,
+            ).start()
+            return carry
+
+        lax.fori_loop(1, devices, deliver, 0)
+        pltpu.make_async_copy(outgoing_ref.at[c, me], out_ref.at[me, :, lanes], self_sem.at[c]).start()
+
+    first = early(0)
+    second = early(1)
+    late(0, first)
+    third = early(2)
+    late(1, second)
+    late(2, third)
+
+    others = pl.ds(0, devices - 1)
+    for c in range(3):
+        for copy in halos[c] + strips[c]:
+            copy.wait_send()
+        lanes = pl.ds(512 * c, 512)
+        pltpu.make_async_copy(outgoing_ref.at[c, me], out_ref.at[me, :, lanes], self_sem.at[c]).wait()
+        pltpu.make_async_copy(outgoing_ref.at[c, others], outgoing_ref.at[c, others], out_send.at[c]).wait()
+        pltpu.make_async_copy(out_ref.at[others, :, lanes], out_ref.at[others, :, lanes], out_recv.at[c]).wait()
 
 
 VMEM = pl.BlockSpec(memory_space=pltpu.VMEM)
 SMEM = pl.BlockSpec(memory_space=pltpu.SMEM)
-
-
-def front(noise, low, high, wall_scale, span_scale, n_wall):
-    return pl.pallas_call(
-        functools.partial(front_kernel, n_wall),
-        out_shape=(
-            jax.ShapeDtypeStruct((3, 128, 2048), F32),
-            jax.ShapeDtypeStruct((3, 48, 2048), BF16),
-            jax.ShapeDtypeStruct((3, 48, 2048), BF16),
-        ),
-        in_specs=[SMEM, SMEM, VMEM, VMEM, VMEM],
-        out_specs=(VMEM, VMEM, VMEM),
-        scratch_shapes=[pltpu.VMEM((16, 16, 8, 128), F32)],
-        name="front",
-    )(wall_scale, span_scale, noise, low, high)
-
-
-def back(centre, left, right, fac, owner, span_scale, devices, slots):
-    return pl.pallas_call(
-        functools.partial(back_kernel, devices, slots),
-        out_shape=jax.ShapeDtypeStruct((devices * slots, 1536), BF16),
-        in_specs=[SMEM, VMEM, VMEM, VMEM, VMEM, VMEM],
-        out_specs=VMEM,
+ANY = pl.BlockSpec(memory_space=pl.ANY)
+MESH = pl.DeviceIdType.MESH
+
+
+def per_device(noise, wall_scale, span_scale, lund_factor, mean_velocity, owner_map):
+    n_span, n_wall = lax.axis_size("span"), lax.axis_size("wall")
+    devices = n_span * n_wall
+    slots = 8
+    received = pl.pallas_call(
+        functools.partial(kernel, n_span, n_wall, slots),
+        out_shape=jax.ShapeDtypeStruct((devices, slots, 1536), BF16),
+        in_specs=[SMEM, SMEM, ANY, VMEM, VMEM, VMEM],
+        out_specs=ANY,
         scratch_shapes=[
-            pltpu.VMEM((2, 128, 2048), F32),
+            pltpu.VMEM(noise.shape, BF16),
+            pltpu.VMEM((3, 32, HALO, 128), BF16),
+            pltpu.VMEM((3, 32, HALO, 128), BF16),
+            pltpu.VMEM((16, 16, 8, 128), F32),
+            pltpu.VMEM((3, 128, 2048), F32),
+            pltpu.VMEM((3, 2 * HALO, 2048), BF16),
+            pltpu.VMEM((3, 2 * HALO, 2048), BF16),
+            pltpu.VMEM((3, 2 * HALO, 2048), BF16),
+            pltpu.VMEM((3, 2 * HALO, 2048), BF16),
+            pltpu.VMEM((8, 64), F32),
             pltpu.VMEM((8, 2048), F32),
             pltpu.VMEM((devices * slots, 512), BF16),
             pltpu.VMEM((512, 512), BF16),
+            pltpu.VMEM((512, 512), BF16),
+            pltpu.VMEM((3, devices, slots, 512), BF16),
+            pltpu.SemaphoreType.DMA((3,)),
+            pltpu.SemaphoreType.DMA((3, 2)),
+            pltpu.SemaphoreType.DMA((3, 2)),
+            pltpu.SemaphoreType.DMA((3, 2)),
+            pltpu.SemaphoreType.DMA((3, 2)),
+            pltpu.SemaphoreType.DMA((3,)),
+            pltpu.SemaphoreType.DMA((3,)),
+            pltpu.SemaphoreType.DMA((3,)),
         ],
-        name="back",
-    )(span_scale, centre, left, right, fac, owner)
-
-
-def per_device(noise, wall_scale, span_scale, lund_factor, mean_velocity, owner_map):
-    planes, rows = noise.shape[1:3]
-    n_span, n_wall = lax.axis_size("span"), lax.axis_size("wall")
-    devices = n_span * n_wall
-    slots = 8
-    up = [(i, (i + 1) % n_wall) for i in range(n_wall)]
-    down = [(b, a) for a, b in up]
-    low = lax.ppermute(noise[:, :, rows - HALO :], "wall", up)
-    high = lax.ppermute(noise[:, :, :HALO], "wall", down)
-    fac = jnp.concatenate([lund_factor, mean_velocity[None], jnp.zeros((1, rows), F32)], axis=0)
-    centre, to_next, to_prev = front(
-        noise, low.reshape(-1, 128), high.reshape(-1, 128), wall_scale, span_scale, n_wall
-    )
-    ahead = [(i, (i + 1) % n_span) for i in range(n_span)]
-    left = lax.ppermute(to_next, "span", ahead)
-    right = lax.ppermute(to_prev, "span", [(b, a) for a, b in ahead])
-    outgoing = back(centre, left, right, fac, owner_map.reshape(1, -1), span_scale, devices, slots)
-    received = lax.all_to_all(
-        outgoing.reshape(devices, slots, -1), ("span", "wall"), split_axis=0, concat_axis=0, tiled=True
+        compiler_params=pltpu.CompilerParams(collective_id=0, has_side_effects=True, vmem_limit_bytes=60 << 20),
+        name="inflow",
+    )(
+        wall_scale, span_scale, noise, lund_factor, mean_velocity.reshape(1, -1), owner_map.reshape(1, -1)
     )
     return received.reshape(1, devices * slots, -1)
 

time: 108 us -> 86.4 us (0.80)
  the two profiles are of different devices: /device:TPU:1 before, /device:TPU:3 now
where the time goes in v2:
time: 86.4 us; the launch traced here: 86.2 us
  Pallas kernels  82.4 us (95%)
  local copies, waits for them, and re-layouts  3.76 us (4%)
    pallas_call x1, Pallas kernels, per_device(): pl.pallas_call(functools.partial(kernel, n_span, n_wall, slots), out_shap...  82.4 us
    unnamed x1, local copies, waits for them, and re-layouts  3.76 us

profile of v2, /device:TPU:3, one launch (start us, length us, event | category | flops | bytes accessed | tf_op | source)
XLA Modules:
  0.0 86.2 jit_solution(7126099961165880819)
XLA Ops:
  0.0 82.4 %inflow.1 = bf16[128,8,1536]{2,1,0:T(8,128)(2,1)} custom-call(f32[3]{0:T(128)} %wscale.1, f32[3]{0:T(128)} %sscale.1, bf16[3,32,64,128]{3,2,1,0:T(8,128)(2,1)} %noise_hbm.1, f32[6,64]{1,0:T(8,128)} %lund_ref.1, f32[1,64]{1,0:T(1,128)} %bitcast.5, s32[1,512]{1,0:T(1,128)} %bitcast.4), custom_call_target="tpu_custom_call" | custom-call | tf_op jit(solution)/shard_map/inflow/pallas_call | solution.py:316
  82.4 3.8 %copy.8 = bf16[1,1024,1536]{2,1,0:T(8,128)(2,1)} copy(bf16[1,1024,1536]{2,1,0:T(8,128)(2,1)} %bitcast.3) | data formatting | bytes 6291456

commit v3 on v2

--- a/solution.py
+++ b/solution.py
@@ -10,6 +10,7 @@
 
 HALO = 24
 EDGE = 4
+STRIP = 32
 F32 = jnp.float32
 BF16 = jnp.bfloat16
 
@@ -73,11 +74,12 @@
     r, k = iota(shape, 0), iota(shape, 1)
     z = EDGE * (r & 31) + (r >> 5)
     hi, lo = split(tap_values(k - z, r >= 0, coefficients))
-    row, col = iota((96, 256), 0), iota((96, 256), 1)
-    g = (row >= 24).astype(jnp.int32) + (row >= 48).astype(jnp.int32) + (row >= 72).astype(jnp.int32)
-    inner = row - HALO * g
-    source = inner + jnp.where(g < 2, 128 - HALO, 0) + 128 * (g & 1)
-    pick = jnp.where(col == source, 1.0, 0.0).astype(BF16)
+    row, col = iota((2 * STRIP, 256), 0), iota((2 * STRIP, 256), 1)
+    j = row & (STRIP - 1)
+    low_term = j >= HALO
+    to_next = jnp.where(low_term, 256 - STRIP + j, 128 - HALO + j)
+    to_prev = jnp.where(low_term, 128 - HALO + j, j)
+    pick = jnp.where(col == jnp.where(row < STRIP, to_next, to_prev), 1.0, 0.0).astype(BF16)
     own = jnp.concatenate(
         [
             jnp.concatenate([hi, hi], axis=1),
@@ -86,16 +88,12 @@
         ],
         axis=0,
     )
-    shape = (128, 192)
-    r, k = iota(shape, 0), iota(shape, 1)
-    z = EDGE * (r & 31) + (r >> 5)
-    second = k >= 96
-    j = jnp.where(second, k - 96, k)
-    right = j >= 48
-    j = jnp.where(right, j - 48, j)
+    second = k >= 2 * STRIP
+    j = k & (STRIP - 1)
     low_term = j >= HALO
-    j = jnp.where(low_term, j - HALO, j)
-    column = jnp.where(right, 128 + j, j - HALO)
+    from_left = jnp.where(low_term, j - STRIP, j - HALO)
+    from_right = jnp.where(low_term, 128 + j - HALO, 128 + j)
+    column = jnp.where((k & STRIP) > 0, from_right, from_left)
     values = tap_values(column - z, r >= 0, coefficients)
     hi = values.astype(BF16).astype(F32)
     strips = jnp.where(second, jnp.where(low_term, 0.0, values - hi), hi).astype(BF16)
@@ -129,8 +127,8 @@
         out = dot_nt(own, jnp.concatenate([hi, lo], axis=1))
         lanes = slice(256 * g, 256 * g + 256)
         psi_ref[c, :, lanes] = out[:128] + out[128:256]
-        to_next_ref[c, :, lanes] = out[256:304].astype(BF16)
-        to_prev_ref[c, :, lanes] = out[304:352].astype(BF16)
+        to_next_ref[c, :, lanes] = out[256 : 256 + STRIP].astype(BF16)
+        to_prev_ref[c, :, lanes] = out[256 + STRIP :].astype(BF16)
 
 
 def lane_factors(fac):
@@ -193,7 +191,7 @@
     n_span, n_wall, slots, wscale, sscale, noise_hbm, lund_ref, mean_ref, owner_ref, out_ref,
     noise_ref, low_ref, high_ref, smooth_ref, psi_ref, to_next_ref, to_prev_ref, left_ref, right_ref,
     fac_ref, lanes_ref, hot_ref, interleave_ref, tile_ref, outgoing_ref,
-    load_sem, halo_send, halo_recv, strip_send, strip_recv, out_send, out_recv, self_sem,
+    load_sem, halo_send, halo_recv, strip_send, strip_recv, out_send, out_recv, self_sem, ready_sem,
 ):
     devices = n_span * n_wall
     span, wall = lax.axis_index("span"), lax.axis_index("wall")
@@ -203,23 +201,18 @@
     def place(index):
         return {"span": lax.div(index, n_wall), "wall": lax.rem(index, n_wall)}
 
+    def greet(sem, axis, size, distance):
+        here = lax.axis_index(axis)
+        for step in (distance, size - distance):
+            pl.semaphore_signal(sem, inc=1, device_id={axis: lax.rem(here + step, size)}, device_id_type=MESH)
+
     barrier = pltpu.get_barrier_semaphore()
-
-    def greet(i, carry):
-        pl.semaphore_signal(barrier, inc=1, device_id=place(jnp.bitwise_xor(me, i)), device_id_type=MESH)
-        return carry
-
-    lax.fori_loop(1, devices, greet, 0)
+    greet(barrier, "wall", n_wall, 1)
+    greet(barrier, "span", n_span, 1)
 
     loads = [pltpu.make_async_copy(noise_hbm.at[c], noise_ref.at[c], load_sem.at[c]) for c in range(3)]
     for load in loads:
         load.start()
-    fac_ref[...] = jnp.zeros_like(fac_ref)
-    fac_ref[0:6] = lund_ref[...]
-    fac_ref[6:7] = mean_ref[...]
-    lanes_ref[...] = lane_factors(fac_ref[...])
-    hot_ref[...] = slot_onehot(owner_ref[...], devices, slots)
-    interleave_ref[...] = interleave_matrix()
 
     def sends(c, step, size, axis, pairs, send_sem, recv_sem):
         here = lax.axis_index(axis)
@@ -252,17 +245,36 @@
         for c in range(3)
     ]
 
-    pl.semaphore_wait(barrier, devices - 1)
+    pl.semaphore_wait(barrier, 4)
+    inner = (wall < n_wall - 1, wall > 0)
+    fed = (wall > 0, wall < n_wall - 1)
     for c in range(3):
-        for copy in halos[c]:
-            copy.start()
+        for i in range(2):
+            pl.when(inner[i])(halos[c][i].start)
+    greet(ready_sem.at[0], "wall", n_wall, 1)
+    greet(ready_sem.at[0], "span", n_span, 1)
+    for i, ref in enumerate((low_ref, high_ref)):
+
+        @pl.when(jnp.logical_not(fed[i]))
+        def _(ref=ref):
+            ref[...] = jnp.zeros_like(ref)
+
+    fac_ref[...] = jnp.zeros_like(fac_ref)
+    fac_ref[0:6] = lund_ref[...]
+    fac_ref[6:7] = mean_ref[...]
+    lanes_ref[...] = lane_factors(fac_ref[...])
+    hot_ref[...] = slot_onehot(owner_ref[...], devices, slots)
+    interleave_ref[...] = interleave_matrix()
+    pl.semaphore_wait(ready_sem.at[0], 4)
+    greet(ready_sem.at[1], "wall", n_wall, 2)
+    greet(ready_sem.at[1], "span", n_span, 2)
 
     def early(c):
         operand = wall_operand(wscale[c], wall, n_wall)
         own, from_strips = span_operands(sscale[c])
         loads[c].wait()
-        for copy in halos[c]:
-            copy.wait_recv()
+        for i in range(2):
+            pl.when(fed[i])(halos[c][i].wait_recv)
         wall_pass(c, noise_ref, low_ref, high_ref, operand, smooth_ref)
         span_own_pass(c, own, smooth_ref, psi_ref, to_next_ref, to_prev_ref)
         for copy in strips[c]:
@@ -274,9 +286,11 @@
             copy.wait_recv()
         finish(c, from_strips, left_ref, right_ref, psi_ref, lanes_ref, hot_ref, interleave_ref, tile_ref, outgoing_ref)
         lanes = pl.ds(512 * c, 512)
+        if c == 0:
+            pl.semaphore_wait(ready_sem.at[3], n_wall - 1)
 
         def deliver(i, carry):
-            to = jnp.bitwise_xor(me, i)
+            to = jnp.bitwise_xor(me, jnp.bitwise_and(37 * i, devices - 1))
             pltpu.make_async_remote_copy(
                 src_ref=outgoing_ref.at[c, to], dst_ref=out_ref.at[me, :, lanes],
                 send_sem=out_send.at[c], recv_sem=out_recv.at[c], device_id=place(to), device_id_type=MESH,
@@ -287,16 +301,24 @@
         pltpu.make_async_copy(outgoing_ref.at[c, me], out_ref.at[me, :, lanes], self_sem.at[c]).start()
 
     first = early(0)
+    pl.semaphore_wait(ready_sem.at[1], 4)
+    greet(ready_sem.at[2], "span", n_span, 4)
     second = early(1)
+    pl.semaphore_wait(ready_sem.at[2], 2)
+    for i in range(1, n_wall):
+        pl.semaphore_signal(
+            ready_sem.at[3], inc=1, device_id={"wall": lax.rem(wall + i, n_wall)}, device_id_type=MESH
+        )
+    third = early(2)
     late(0, first)
-    third = early(2)
     late(1, second)
     late(2, third)
 
     others = pl.ds(0, devices - 1)
     for c in range(3):
-        for copy in halos[c] + strips[c]:
-            copy.wait_send()
+        for i in range(2):
+            pl.when(inner[i])(halos[c][i].wait_send)
+            strips[c][i].wait_send()
         lanes = pl.ds(512 * c, 512)
         pltpu.make_async_copy(outgoing_ref.at[c, me], out_ref.at[me, :, lanes], self_sem.at[c]).wait()
         pltpu.make_async_copy(outgoing_ref.at[c, others], outgoing_ref.at[c, others], out_send.at[c]).wait()
@@ -324,10 +346,10 @@
             pltpu.VMEM((3, 32, HALO, 128), BF16),
             pltpu.VMEM((16, 16, 8, 128), F32),
             pltpu.VMEM((3, 128, 2048), F32),
-            pltpu.VMEM((3, 2 * HALO, 2048), BF16),
-            pltpu.VMEM((3, 2 * HALO, 2048), BF16),
-            pltpu.VMEM((3, 2 * HALO, 2048), BF16),
-            pltpu.VMEM((3, 2 * HALO, 2048), BF16),
+            pltpu.VMEM((3, STRIP, 2048), BF16),
+            pltpu.VMEM((3, STRIP, 2048), BF16),
+            pltpu.VMEM((3, STRIP, 2048), BF16),
+            pltpu.VMEM((3, STRIP, 2048), BF16),
             pltpu.VMEM((8, 64), F32),
             pltpu.VMEM((8, 2048), F32),
             pltpu.VMEM((devices * slots, 512), BF16),
@@ -342,6 +364,7 @@
             pltpu.SemaphoreType.DMA((3,)),
             pltpu.SemaphoreType.DMA((3,)),
             pltpu.SemaphoreType.DMA((3,)),
+            pltpu.SemaphoreType.REGULAR((4,)),
         ],
         compiler_params=pltpu.CompilerParams(collective_id=0, has_side_effects=True, vmem_limit_bytes=60 << 20),
         name="inflow",

time: 86.4 us -> 70.7 us (0.82)
  the two profiles are of different devices: /device:TPU:3 before, /device:TPU:1 now
where the time goes in v3:
time: 70.7 us; the launch traced here: 70.6 us
  Pallas kernels  66.8 us (94%)
  local copies, waits for them, and re-layouts  3.76 us (5%)
    pallas_call x1, Pallas kernels, per_device(): pl.pallas_call(functools.partial(kernel, n_span, n_wall, slots), out_shap...  66.8 us
    unnamed x1, local copies, waits for them, and re-layouts  3.76 us

profile of v3, /device:TPU:1, one launch (start us, length us, event | category | flops | bytes accessed | tf_op | source)
XLA Modules:
  0.0 70.6 jit_solution(6540950771877852145)
XLA Ops:
  0.0 66.8 %inflow.1 = bf16[128,8,1536]{2,1,0:T(8,128)(2,1)} custom-call(f32[3]{0:T(128)} %wscale.1, f32[3]{0:T(128)} %sscale.1, bf16[3,32,64,128]{3,2,1,0:T(8,128)(2,1)} %noise_hbm.1, f32[6,64]{1,0:T(8,128)} %lund_ref.1, f32[1,64]{1,0:T(1,128)} %bitcast.5, s32[1,512]{1,0:T(1,128)} %bitcast.4), custom_call_target="tpu_custom_call" | custom-call | tf_op jit(solution)/shard_map/inflow/pallas_call | solution.py:338
  66.8 3.8 %copy.8 = bf16[1,1024,1536]{2,1,0:T(8,128)(2,1)} copy(bf16[1,1024,1536]{2,1,0:T(8,128)(2,1)} %bitcast.3) | data formatting | bytes 6291456

commit v4 on v3

--- a/solution.py
+++ b/solution.py
@@ -10,7 +10,6 @@
 
 HALO = 24
 EDGE = 4
-STRIP = 32
 F32 = jnp.float32
 BF16 = jnp.bfloat16
 
@@ -74,30 +73,24 @@
     r, k = iota(shape, 0), iota(shape, 1)
     z = EDGE * (r & 31) + (r >> 5)
     hi, lo = split(tap_values(k - z, r >= 0, coefficients))
-    row, col = iota((2 * STRIP, 256), 0), iota((2 * STRIP, 256), 1)
-    j = row & (STRIP - 1)
-    low_term = j >= HALO
-    to_next = jnp.where(low_term, 256 - STRIP + j, 128 - HALO + j)
-    to_prev = jnp.where(low_term, 128 - HALO + j, j)
-    pick = jnp.where(col == jnp.where(row < STRIP, to_next, to_prev), 1.0, 0.0).astype(BF16)
+    row, col = iota((2 * HALO, 256), 0), iota((2 * HALO, 256), 1)
+    source = jnp.where(row < HALO, 128 - HALO + row, row - HALO)
     own = jnp.concatenate(
         [
             jnp.concatenate([hi, hi], axis=1),
             jnp.concatenate([lo, jnp.zeros_like(lo)], axis=1),
-            pick,
+            jnp.where(col == source, 1.0, 0.0).astype(BF16),
         ],
         axis=0,
     )
-    second = k >= 2 * STRIP
-    j = k & (STRIP - 1)
-    low_term = j >= HALO
-    from_left = jnp.where(low_term, j - STRIP, j - HALO)
-    from_right = jnp.where(low_term, 128 + j - HALO, 128 + j)
-    column = jnp.where((k & STRIP) > 0, from_right, from_left)
-    values = tap_values(column - z, r >= 0, coefficients)
-    hi = values.astype(BF16).astype(F32)
-    strips = jnp.where(second, jnp.where(low_term, 0.0, values - hi), hi).astype(BF16)
-    return own, strips
+    shape = (128, 4 * HALO)
+    r, k = iota(shape, 0), iota(shape, 1)
+    z = EDGE * (r & 31) + (r >> 5)
+    second = k >= 2 * HALO
+    j = jnp.where(second, k - 2 * HALO, k)
+    column = jnp.where(j >= HALO, 128 + j - HALO, j - HALO)
+    hi, lo = split(tap_values(column - z, r >= 0, coefficients))
+    return own, jnp.where(second, lo.astype(F32), hi.astype(F32)).astype(BF16)
 
 
 def wall_pass(c, noise_ref, low_ref, high_ref, operand, smooth_ref):
@@ -127,8 +120,8 @@
         out = dot_nt(own, jnp.concatenate([hi, lo], axis=1))
         lanes = slice(256 * g, 256 * g + 256)
         psi_ref[c, :, lanes] = out[:128] + out[128:256]
-        to_next_ref[c, :, lanes] = out[256 : 256 + STRIP].astype(BF16)
-        to_prev_ref[c, :, lanes] = out[256 + STRIP :].astype(BF16)
+        to_next_ref[c, :, lanes] = out[256 : 256 + HALO].astype(BF16)
+        to_prev_ref[c, :, lanes] = out[256 + HALO :].astype(BF16)
 
 
 def lane_factors(fac):
@@ -290,7 +283,7 @@
             pl.semaphore_wait(ready_sem.at[3], n_wall - 1)
 
         def deliver(i, carry):
-            to = jnp.bitwise_xor(me, jnp.bitwise_and(37 * i, devices - 1))
+            to = jnp.bitwise_xor(me, jnp.bitwise_and(43 * i, devices - 1))
             pltpu.make_async_remote_copy(
                 src_ref=outgoing_ref.at[c, to], dst_ref=out_ref.at[me, :, lanes],
                 send_sem=out_send.at[c], recv_sem=out_recv.at[c], device_id=place(to), device_id_type=MESH,
@@ -346,10 +339,10 @@
             pltpu.VMEM((3, 32, HALO, 128), BF16),
             pltpu.VMEM((16, 16, 8, 128), F32),
             pltpu.VMEM((3, 128, 2048), F32),
-            pltpu.VMEM((3, STRIP, 2048), BF16),
-            pltpu.VMEM((3, STRIP, 2048), BF16),
-            pltpu.VMEM((3, STRIP, 2048), BF16),
-            pltpu.VMEM((3, STRIP, 2048), BF16),
+            pltpu.VMEM((3, HALO, 2048), BF16),
+            pltpu.VMEM((3, HALO, 2048), BF16),
+            pltpu.VMEM((3, HALO, 2048), BF16),
+            pltpu.VMEM((3, HALO, 2048), BF16),
             pltpu.VMEM((8, 64), F32),
             pltpu.VMEM((8, 2048), F32),
             pltpu.VMEM((devices * slots, 512), BF16),

time: 70.7 us -> 68.9 us (0.975)
  Pallas kernels: 66.8 us -> 65 us
    pallas_call x1, Pallas kernels: 66.8 us -> 65 us  [per_device(): pl.pallas_call(functools.partial(kernel, n_span, n_wall, slots), out_shap...]
where the time goes in v4:
time: 68.9 us; the launch traced here: 68.8 us
  Pallas kernels  65 us (94%)
  local copies, waits for them, and re-layouts  3.76 us (5%)
    pallas_call x1, Pallas kernels, per_device(): pl.pallas_call(functools.partial(kernel, n_span, n_wall, slots), out_shap...  65 us
    unnamed x1, local copies, waits for them, and re-layouts  3.76 us

profile of v4, /device:TPU:1, one launch (start us, length us, event | category | flops | bytes accessed | tf_op | source)
XLA Modules:
  0.0 68.8 jit_solution(4332620084044848909)
XLA Ops:
  0.0 65.0 %inflow.1 = bf16[128,8,1536]{2,1,0:T(8,128)(2,1)} custom-call(f32[3]{0:T(128)} %wscale.1, f32[3]{0:T(128)} %sscale.1, bf16[3,32,64,128]{3,2,1,0:T(8,128)(2,1)} %noise_hbm.1, f32[6,64]{1,0:T(8,128)} %lund_ref.1, f32[1,64]{1,0:T(1,128)} %bitcast.5, s32[1,512]{1,0:T(1,128)} %bitcast.4), custom_call_target="tpu_custom_call" | custom-call | tf_op jit(solution)/shard_map/inflow/pallas_call | solution.py:331
  65.0 3.8 %copy.8 = bf16[1,1024,1536]{2,1,0:T(8,128)(2,1)} copy(bf16[1,1024,1536]{2,1,0:T(8,128)(2,1)} %bitcast.3) | data formatting | bytes 6291456

commit v5 on v3

--- a/solution.py
+++ b/solution.py
@@ -290,7 +290,7 @@
             pl.semaphore_wait(ready_sem.at[3], n_wall - 1)
 
         def deliver(i, carry):
-            to = jnp.bitwise_xor(me, jnp.bitwise_and(37 * i, devices - 1))
+            to = jnp.bitwise_xor(me, jnp.bitwise_and(43 * i, devices - 1))
             pltpu.make_async_remote_copy(
                 src_ref=outgoing_ref.at[c, to], dst_ref=out_ref.at[me, :, lanes],
                 send_sem=out_send.at[c], recv_sem=out_recv.at[c], device_id=place(to), device_id_type=MESH,

time: 70.7 us -> 70.9 us (level)
  no operation moved by 1% of the time
where the time goes in v5:
time: 70.9 us; the launch traced here: 70.8 us
  Pallas kernels  67 us (94%)
  local copies, waits for them, and re-layouts  3.76 us (5%)
    pallas_call x1, Pallas kernels, per_device(): pl.pallas_call(functools.partial(kernel, n_span, n_wall, slots), out_shap...  67 us
    unnamed x1, local copies, waits for them, and re-layouts  3.76 us

profile of v5, /device:TPU:1, one launch (start us, length us, event | category | flops | bytes accessed | tf_op | source)
XLA Modules:
  0.0 70.8 jit_solution(16992290292329649987)
XLA Ops:
  0.0 67.0 %inflow.1 = bf16[128,8,1536]{2,1,0:T(8,128)(2,1)} custom-call(f32[3]{0:T(128)} %wscale.1, f32[3]{0:T(128)} %sscale.1, bf16[3,32,64,128]{3,2,1,0:T(8,128)(2,1)} %noise_hbm.1, f32[6,64]{1,0:T(8,128)} %lund_ref.1, f32[1,64]{1,0:T(1,128)} %bitcast.5, s32[1,512]{1,0:T(1,128)} %bitcast.4), custom_call_target="tpu_custom_call" | custom-call | tf_op jit(solution)/shard_map/inflow/pallas_call | solution.py:338
  67.0 3.8 %copy.8 = bf16[1,1024,1536]{2,1,0:T(8,128)(2,1)} copy(bf16[1,1024,1536]{2,1,0:T(8,128)(2,1)} %bitcast.3) | data formatting | bytes 6291456

commit v6 on v4

--- a/solution.py
+++ b/solution.py
@@ -192,7 +192,7 @@
     rows = noise_hbm.shape[2]
 
     def place(index):
-        return {"span": lax.div(index, n_wall), "wall": lax.rem(index, n_wall)}
+        return {"span": index >> (n_wall.bit_length() - 1), "wall": jnp.bitwise_and(index, n_wall - 1)}
 
     def greet(sem, axis, size, distance):
         here = lax.axis_index(axis)

time: 68.9 us -> 68.9 us (level)
  no operation moved by 1% of the time
where the time goes in v6:
time: 68.9 us; the launch traced here: 68.8 us
  Pallas kernels  65 us (94%)
  local copies, waits for them, and re-layouts  3.76 us (5%)
    pallas_call x1, Pallas kernels, per_device(): pl.pallas_call(functools.partial(kernel, n_span, n_wall, slots), out_shap...  65 us
    unnamed x1, local copies, waits for them, and re-layouts  3.76 us

profile of v6, /device:TPU:1, one launch (start us, length us, event | category | flops | bytes accessed | tf_op | source)
XLA Modules:
  0.0 68.8 jit_solution(17706354210834626682)
XLA Ops:
  0.0 65.0 %inflow.1 = bf16[128,8,1536]{2,1,0:T(8,128)(2,1)} custom-call(f32[3]{0:T(128)} %wscale.1, f32[3]{0:T(128)} %sscale.1, bf16[3,32,64,128]{3,2,1,0:T(8,128)(2,1)} %noise_hbm.1, f32[6,64]{1,0:T(8,128)} %lund_ref.1, f32[1,64]{1,0:T(1,128)} %bitcast.5, s32[1,512]{1,0:T(1,128)} %bitcast.4), custom_call_target="tpu_custom_call" | custom-call | tf_op jit(solution)/shard_map/inflow/pallas_call | solution.py:331
  65.0 3.8 %copy.8 = bf16[1,1024,1536]{2,1,0:T(8,128)(2,1)} copy(bf16[1,1024,1536]{2,1,0:T(8,128)(2,1)} %bitcast.3) | data formatting | bytes 6291456
